TPU v7x, 256 devices: a whole 4x4x8 slice. The times are simulated.
256 devices in a mesh: gx: 8 (over y, core), gy: 32 (over x, z).
Axes of the slice: x: 4, y: 4, z: 8, core: 2. Of those that a mesh axis runs over, the one named last changes fastest.
Arguments:
- flow_field: float32 [16, 256, 256, 128], P(None, 'gx', 'gy'), may hold values from -6 to 6
- cotangent: float32 [16, 256, 256, 128], P(None, 'gx', 'gy'), may hold values from -6 to 6
- mode_weights: float32 [4, 16, 16, 256], replicated, may hold values from -3 to 3
- point_weights: float32 [16, 16], replicated, may hold values from -1.5 to 1.5
- point_bias: float32 [16], replicated, may hold values from -3 to 3
Outputs:
- output_field: float32 [16, 256, 256, 128], P(None, 'gx', 'gy')
- grad_field: float32 [16, 256, 256, 128], P(None, 'gx', 'gy')
- grad_modes: float32 [4, 16, 16, 256], replicated
- grad_point: float32 [16, 16], replicated
- grad_bias: float32 [16], replicated
All inputs are finite; a program needn't handle non-finite values.
Results may differ from a plain program's by a relative error of at most 0.00024.
Values sent between devices are 32-bit elements; how exact they have to be, the bound alone decides.
No kernel may reach another device: no remote copies, remote signals or barrier semaphores. Data moves between devices by JAX's collectives and lax.ppermute only.
A program may use at most 128 MiB of HBM per device.

v0:
```python
import math
import jax
import jax.numpy as jnp
from jax import lax
from jax.sharding import PartitionSpec as P

LOW_PASS = [
    0.23037781330885523,
    0.7148465705525415,
    0.6308807679295904,
    -0.02798376941698385,
    -0.18703481171888114,
    0.030841381835986965,
    0.032883011666982945,
    -0.010597401784997278,
]
HIGH_PASS = [(-1) ** position * LOW_PASS[7 - position] for position in range(8)]
GELU_SCALE = 0.7978845608028654
GELU_CUBE = 0.044715


def from_behind(value, axis, by):
    devices = lax.axis_size(axis)
    return lax.ppermute(value, axis, [(i, (i + by) % devices) for i in range(devices)])


def filter_table(filter_taps, out_count, in_count, periodic):
    row_index = lax.broadcasted_iota(jnp.int32, (out_count, in_count), 0)
    col_index = lax.broadcasted_iota(jnp.int32, (out_count, in_count), 1)
    offset = col_index - 2 * row_index
    if periodic:
        offset = offset % in_count
    matrix = jnp.zeros((out_count, in_count), jnp.float32)
    for position in range(8):
        matrix = matrix + filter_taps[position] * (offset == position).astype(jnp.float32)
    return matrix


def lifted_table(filter_taps, out_count, in_count):
    row_index = lax.broadcasted_iota(jnp.int32, (out_count, in_count), 0)
    col_index = lax.broadcasted_iota(jnp.int32, (out_count, in_count), 1)
    offset = row_index - 2 * col_index + 6
    matrix = jnp.zeros((out_count, in_count), jnp.float32)
    for position in range(8):
        matrix = matrix + filter_taps[position] * (offset == position).astype(jnp.float32)
    return matrix


def along_x(matrix, signal):
    return jnp.einsum("kr,arys->akys", matrix, signal, precision=lax.Precision.HIGHEST)


def along_y(matrix, signal):
    return jnp.einsum("kr,axrs->axks", matrix, signal, precision=lax.Precision.HIGHEST)


def plane_x(matrix, signal):
    return jnp.einsum("kr,ary->aky", matrix, signal, precision=lax.Precision.HIGHEST)


def plane_y(matrix, signal):
    return jnp.einsum("kr,axr->axk", matrix, signal, precision=lax.Precision.HIGHEST)


def to_lanes(signal):
    channels, extent_x, extent_y, planes = signal.shape
    return jnp.transpose(signal, (0, 3, 1, 2)).reshape(channels * planes, extent_x, extent_y)


def from_lanes(signal, channels):
    stacked, extent_x, extent_y = signal.shape
    return jnp.transpose(
        signal.reshape(channels, stacked // channels, extent_x, extent_y), (0, 2, 3, 1)
    )


def four_bands(signal):
    extent_x, extent_y = (signal.shape[1], signal.shape[2])
    low_x = plane_x(filter_table(LOW_PASS, extent_x // 2, extent_x, True), signal)
    high_x = plane_x(filter_table(HIGH_PASS, extent_x // 2, extent_x, True), signal)
    low_y = filter_table(LOW_PASS, extent_y // 2, extent_y, True)
    high_y = filter_table(HIGH_PASS, extent_y // 2, extent_y, True)
    return jnp.stack(
        [
            plane_y(low_y, low_x),
            plane_y(low_y, high_x),
            plane_y(high_y, low_x),
            plane_y(high_y, high_x),
        ]
    )


def join_bands(changes):
    modes_x, modes_y = (changes.shape[2], changes.shape[3])
    low_x = filter_table(LOW_PASS, modes_x, 2 * modes_x, True).T
    high_x = filter_table(HIGH_PASS, modes_x, 2 * modes_x, True).T
    low_y = filter_table(LOW_PASS, modes_y, 2 * modes_y, True).T
    high_y = filter_table(HIGH_PASS, modes_y, 2 * modes_y, True).T
    from_low = plane_y(low_y, changes[0]) + plane_y(high_y, changes[2])
    from_high = plane_y(low_y, changes[1]) + plane_y(high_y, changes[3])
    return plane_x(low_x, from_low) + plane_x(high_x, from_high)


def gelu_parts(signal):
    tangent = jnp.tanh(GELU_SCALE * (signal + GELU_CUBE * signal * signal * signal))
    activated = 0.5 * signal * (1.0 + tangent)
    gelu_slope = 0.5 * (1.0 + tangent) + 0.5 * signal * (1.0 - tangent * tangent) * GELU_SCALE * (
        1.0 + 3.0 * GELU_CUBE * signal * signal
    )
    return (activated, gelu_slope)


def wave_block(signal, weights_grid, transposed):
    x_index = lax.axis_index("gx")
    channels = signal.shape[0]
    extent_x, extent_y = (signal.shape[1], signal.shape[2])
    margin = from_behind(signal[:, :6], "gx", -1)
    halved = along_x(
        filter_table(LOW_PASS, extent_x // 2, extent_x + 6, False),
        jnp.concatenate([signal, margin], 1),
    )
    margin = from_behind(halved[:, :, :6], "gy", -1)
    level_one = along_y(
        filter_table(LOW_PASS, extent_y // 2, extent_y + 6, False),
        jnp.concatenate([halved, margin], 2),
    )
    level_one = to_lanes(lax.all_to_all(level_one, "gy", split_axis=3, concat_axis=2, tiled=True))
    rows_one, cols_one = (level_one.shape[1], level_one.shape[2])
    margin = from_behind(level_one[:, :6], "gx", -1)
    level_two = plane_x(
        filter_table(LOW_PASS, rows_one // 2, rows_one + 6, False),
        jnp.concatenate([level_one, margin], 1),
    )
    level_two = plane_y(filter_table(LOW_PASS, cols_one // 2, cols_one, True), level_two)
    rows_two, cols_two = (level_two.shape[1], level_two.shape[2])
    margin = from_behind(level_two[:, :6], "gx", -1)
    level_three = plane_x(
        filter_table(LOW_PASS, rows_two // 2, rows_two + 6, False),
        jnp.concatenate([level_two, margin], 1),
    )
    level_three = plane_y(filter_table(LOW_PASS, cols_two // 2, cols_two, True), level_three)
    gathered = lax.all_gather(level_three, "gx", axis=1, tiled=True)
    wave_bands = four_bands(gathered)
    stacked, modes_x, modes_y = (wave_bands.shape[1], wave_bands.shape[2], wave_bands.shape[3])
    split_bands = wave_bands.reshape(4, channels, stacked // channels, modes_x, modes_y)
    if transposed:
        mixed_bands = jnp.einsum(
            "bozxy,bioxy->bizxy", split_bands, weights_grid, precision=lax.Precision.HIGHEST
        )
    else:
        mixed_bands = jnp.einsum(
            "bizxy,bioxy->bozxy", split_bands, weights_grid, precision=lax.Precision.HIGHEST
        )
    delta_three = join_bands((mixed_bands - split_bands).reshape(4, stacked, modes_x, modes_y))
    own_rows = rows_two // 2
    own_part = lax.dynamic_slice_in_dim(delta_three, x_index * own_rows, own_rows, 1)
    margin = from_behind(own_part[:, own_rows - 3 :], "gx", 1)
    delta_two = plane_x(
        lifted_table(LOW_PASS, 2 * own_rows, own_rows + 3), jnp.concatenate([margin, own_part], 1)
    )
    cols_three = own_part.shape[2]
    delta_two = plane_y(filter_table(LOW_PASS, cols_three, 2 * cols_three, True).T, delta_two)
    margin = from_behind(delta_two[:, rows_two - 3 :], "gx", 1)
    delta_one = plane_x(
        lifted_table(LOW_PASS, 2 * rows_two, rows_two + 3), jnp.concatenate([margin, delta_two], 1)
    )
    delta_one = plane_y(filter_table(LOW_PASS, cols_two, 2 * cols_two, True).T, delta_one)
    returned = lax.all_to_all(
        from_lanes(delta_one, channels), "gy", split_axis=2, concat_axis=3, tiled=True
    )
    rows_back = returned.shape[1]
    margin = from_behind(returned[:, rows_back - 3 :], "gx", 1)
    widened = along_x(
        lifted_table(LOW_PASS, 2 * rows_back, rows_back + 3), jnp.concatenate([margin, returned], 1)
    )
    cols_back = widened.shape[2]
    margin = from_behind(widened[:, :, cols_back - 3 :], "gy", 1)
    delta_zero = along_y(
        lifted_table(LOW_PASS, 2 * cols_back, cols_back + 3), jnp.concatenate([margin, widened], 2)
    )
    return (signal + delta_zero, split_bands)


def local(flow_field, cotangent, mode_weights, point_weights, point_bias):
    channels = flow_field.shape[0]
    modes_x = flow_field.shape[1] * lax.axis_size("gx") // 16
    modes_y = flow_field.shape[2] * lax.axis_size("gy") // 16
    weights_grid = mode_weights.reshape(4, channels, channels, modes_x, modes_y)
    spectral_flow, bands_flow = wave_block(flow_field, weights_grid, False)
    pointwise = jnp.einsum(
        "io,ixys->oxys", point_weights, flow_field, precision=lax.Precision.HIGHEST
    )
    before_gelu = spectral_flow + pointwise + point_bias[:, None, None, None]
    output_field, gelu_slope = gelu_parts(before_gelu)
    grad_inner = cotangent * gelu_slope
    spectral_grad, bands_grad = wave_block(grad_inner, weights_grid, True)
    point_back = jnp.einsum(
        "io,oxys->ixys", point_weights, grad_inner, precision=lax.Precision.HIGHEST
    )
    grad_field = spectral_grad + point_back
    mode_local = jnp.einsum(
        "bizxy,bozxy->bioxy", bands_flow, bands_grad, precision=lax.Precision.HIGHEST
    )
    mode_local = mode_local.reshape(4, channels, channels, modes_x * modes_y)
    mode_total = lax.psum(mode_local, "gy")
    point_local = jnp.einsum(
        "ixys,oxys->io", flow_field, grad_inner, precision=lax.Precision.HIGHEST
    )
    bias_local = jnp.sum(grad_inner, axis=(1, 2, 3))
    point_total, bias_total = lax.psum((point_local, bias_local), ("gx", "gy"))
    plane_total = flow_field.shape[3]
    cell_count = (
        plane_total
        * flow_field.shape[1]
        * flow_field.shape[2]
        * lax.axis_size("gx")
        * lax.axis_size("gy")
    )
    grad_modes = mode_total / math.sqrt(plane_total)
    grad_point = point_total / math.sqrt(cell_count)
    grad_bias = bias_total / math.sqrt(cell_count)
    return (output_field, grad_field, grad_modes, grad_point, grad_bias)


def solution(mesh):
    in_specs = (P(None, "gx", "gy", None), P(None, "gx", "gy", None), P(), P(), P())
    out_specs = (P(None, "gx", "gy", None), P(None, "gx", "gy", None), P(), P(), P())
    return jax.shard_map(local, mesh=mesh, in_specs=in_specs, out_specs=out_specs, check_vma=False)
```

profile of v0, /device:TPU:8, one launch (start us, length us, event | category | flops | bytes accessed | tf_op | source)
XLA Modules:
  0.0 609.2 jit_solution(3356555167298708479)
XLA Ops:
  7.2 2.0 copy.207
  9.3 6.7 %collective-permute-done = f32[16,6,8,128]{3,1,2,0:T(8,128)S(1)} collective-permute-done((f32[16,6,8,128]{3,1,2,0:T(8,128)S(1)}, f32[16,6,8,128]{3,1,2,0:T(8,128)S(1)}, u32[]{:S(2)}, u32[]{:S(2)}) %collective-permute-start) | collective-permute-done | bytes 393248 | tf_op jit(solution)/shard_map/ppermute | solution.py:24
  17.9 8.1 %collective-permute-start.1 = (f32[16,16,6,128]{3,1,2,0:T(8,128)S(1)}, f32[16,16,6,128]{3,1,2,0:T(8,128)S(1)}, u32[]{:S(2)}, u32[]{:S(2)}) collective-permute-start(f32[16,16,6,128]{3,1,2,0:T(8,128)S(1)} %slice.105), channel_id=1, source_target_pairs={{0,31},{1,0},{2,1},{3,2},{4,3},{5,4},{6,5},{7,6},{8,7},{9,8},{10,9... | collective-permute-start | bytes 2359304 | tf_op jit(solution)/shard_map/ppermute | solution.py:24
  26.0 17.1 %collective-permute-done.1 = f32[16,16,6,128]{3,1,2,0:T(8,128)S(1)} collective-permute-done((f32[16,16,6,128]{3,1,2,0:T(8,128)S(1)}, f32[16,16,6,128]{3,1,2,0:T(8,128)S(1)}, u32[]{:S(2)}, u32[]{:S(2)}) %collective-permute-start.1) | collective-permute-done | bytes 786464 | tf_op jit(solution)/shard_map/ppermute | solution.py:24
  43.2 2.1 fusion.39
  45.4 4.4 copy.209
  49.8 4.3 reshape.86
  54.1 7.6 %all-to-all-start = ((f32[32,1,4096]{2,1,0:T(1,128)}), f32[32,1,4096]{2,1,0:T(1,128)S(1)}, u32[]{:S(2)}, u32[]{:S(2)}) async-start(f32[32,1,4096]{2,1,0:T(1,128)} %reshape.86), calls=%async_computation | async-start | bytes 1048576 | tf_op jit(solution)/shard_map/all_to_all | solution.py:127
  61.7 6.2 %copy.304 = f32[4,16,16,256]{2,1,3,0:T(8,128)} copy(f32[4,16,16,256]{3,2,1,0:T(8,128)S(1)} %copy-done.4) | data formatting | bytes 2097152 | tf_op jit(solution)/shard_map/reshape | solution.py:188
  68.0 11.4 %all-to-all-done = f32[32,1,4096]{2,1,0:T(1,128)S(1)} async-done(((f32[32,1,4096]{2,1,0:T(1,128)}), f32[32,1,4096]{2,1,0:T(1,128)S(1)}, u32[]{:S(2)}, u32[]{:S(2)}) %all-to-all-start) | async-done | bytes 524320 | tf_op jit(solution)/shard_map/all_to_all | solution.py:127
  81.8 2.8 reshape.87
  84.6 4.8 copy.211
  89.4 3.7 copy.212
  93.2 3.9 collective-permute-done.2
  100.1 3.9 collective-permute-done.3
  105.0 14.3 %all_gather.6 = f32[64,32,32]{0,2,1:T(8,128)S(1)} all-gather(f32[64,4,32]{0,2,1:T(8,128)S(1)} %fusion.123), channel_id=1, replica_groups=mesh['gx'=8,'gy'=32] {'gx'}, dimensions={1}, use_global_device_ids=true | all-gather | bytes 294912 | tf_op jit(solution)/shard_map/all_gather | solution.py:142
  125.7 14.9 %bitcast_subtract_fusion.1 = f32[4,16,4,16,16]{1,2,4,3,0:T(4,128)S(1)} fusion(f32[4,16,16,16,16]{2,1,4,3,0:T(8,128)} %bitcast.264, f32[1,16,4,16,16]{1,2,4,3,0:T(4,128)S(1)} %copy.227, f32[1,16,4,16,16]{1,2,4,3,0:T(4,128)S(1)} %copy.226, f32[1,16,4,16,16]{1,2,4,3,0:T(4,128)S(1)} %copy.225, f32[1,16,4,16,16]{1,2,4,3,0:T(4,128)S(1)} %copy.224), kind=kOutput, calls=%fused_computation.23 | convolution fusion | flops 13041664 | bytes 1572864 | tf_op jit(solution)/shard_map/bizxy,bioxy->bozxy/dot_general | solution.py:151
  150.9 4.8 collective-permute-done.4
  156.7 4.0 collective-permute-done.5
  162.3 4.4 copy.241
  166.7 4.8 bitcast_bitcast_fusion.1
  171.5 3.5 reshape.88
  175.0 22.0 %all_to_all.72 = f32[32,1,4096]{2,1,0:T(1,128)S(1)} all-to-all(f32[32,1,4096]{2,1,0:T(1,128)S(1)} %reshape.88), channel_id=1, replica_groups=mesh['gx'=8,'gy'=32] {'gy'}, dimensions={0} | all-to-all | bytes 1048576 | tf_op jit(solution)/shard_map/all_to_all | solution.py:168
  199.0 2.8 reshape.89
  201.8 4.7 copy.242
  206.5 2.8 copy.243
  209.4 4.4 collective-permute-done.6
  214.9 2.2 collective-permute-start.7
  217.2 2.8 fusion.27
  220.1 15.0 %collective-permute-done.7 = f32[16,32,3,128]{3,1,2,0:T(8,128)S(1)} collective-permute-done((f32[16,32,3,128]{3,1,2,0:T(8,128)S(1)}, f32[16,32,3,128]{3,1,2,0:T(8,128)S(1)}, u32[]{:S(2)}, u32[]{:S(2)}) %collective-permute-start.7) | collective-permute-done | bytes 786464 | tf_op jit(solution)/shard_map/ppermute | solution.py:24
  235.3 6.6 %fusion.1133 = (f32[16]{0:T(128)}, f32[16,32,8,128]{3,2,1,0:T(8,128)S(1)}, f32[16,32,8,128]{3,2,1,0:T(8,128)}) fusion(f32[16,32,8,128]{3,2,1,0:T(8,128)S(1)} %copy-done.20, f32[16]{0:T(128)S(1)} %copy-done.21, f32[16,32,8,128]{3,0,2,1:T(8,128)S(1)} %fusion.27, f32[16,32,8,128]{3,2,1,0:T(8,128)S(1)} %copy-done.1, s32[7]{0:T(128)S(1)} %iota_multiply_fusion.2, ...), kind=kOutput, calls=%fused_computation.1198 | convolution fusion | flops 56100200 | bytes 12320924 | tf_op jit(solution)/shard_map/kr,axrs->axks/dot_general | solution.py:54
  241.9 5.3 collective-permute-done.8
  247.4 2.0 fusion.33
  249.6 19.6 %collective-permute-done.9 = f32[16,16,6,128]{3,1,2,0:T(8,128)S(1)} collective-permute-done((f32[16,16,6,128]{3,1,2,0:T(8,128)S(1)}, f32[16,16,6,128]{3,1,2,0:T(8,128)S(1)}, u32[]{:S(2)}, u32[]{:S(2)}) %collective-permute-start.9) | collective-permute-done | bytes 786464 | tf_op jit(solution)/shard_map/ppermute | solution.py:24
  269.3 2.1 fusion.42
  271.5 4.4 copy.251
  275.9 3.5 reshape.90
  279.4 19.5 %all_to_all.73 = f32[32,1,4096]{2,1,0:T(1,128)S(1)} all-to-all(f32[32,1,4096]{2,1,0:T(1,128)S(1)} %reshape.90), channel_id=1, replica_groups=mesh['gx'=8,'gy'=32] {'gy'}, dimensions={0} | all-to-all | bytes 1048576 | tf_op jit(solution)/shard_map/all_to_all | solution.py:127
  300.8 2.8 reshape.91
  303.6 4.8 copy.253
  308.4 3.7 copy.254
  312.2 3.9 collective-permute-done.10
  319.1 5.1 collective-permute-done.11
  325.1 17.3 %all_gather.7 = f32[64,32,32]{0,2,1:T(8,128)S(1)} all-gather(f32[64,4,32]{0,2,1:T(8,128)S(1)} %fusion.119), channel_id=1, replica_groups=mesh['gx'=8,'gy'=32] {'gx'}, dimensions={1}, use_global_device_ids=true | all-gather | bytes 294912 | tf_op jit(solution)/shard_map/all_gather | solution.py:142
  350.4 18.2 %bitcast_subtract_fusion = f32[4,16,4,16,16]{1,2,4,3,0:T(4,128)S(1)} fusion(f32[4,16,16,16,16]{2,1,4,3,0:T(8,128)} %bitcast.265, f32[1,16,4,16,16]{1,2,4,3,0:T(4,128)} %copy.269, f32[1,16,4,16,16]{1,2,4,3,0:T(4,128)} %copy.268, f32[1,16,4,16,16]{1,2,4,3,0:T(4,128)} %copy.267, f32[1,16,4,16,16]{1,2,4,3,0:T(4,128)S(1)} %copy.266), kind=kOutput, calls=%fused_computation.19 | convolution fusion | flops 13041664 | bytes 1572864 | tf_op jit(solution)/shard_map/bozxy,bioxy->bizxy/dot_general | solution.py:147
  384.9 4.8 collective-permute-done.12
  390.7 4.0 collective-permute-done.13
  396.3 4.4 copy.283
  400.7 4.7 bitcast_bitcast_fusion
  405.5 4.2 reshape.92
  409.7 5.7 all-to-all-start.3
  415.5 17.6 %fusion.86 = f32[4,16,16,16,16]{4,3,2,1,0:T(8,128)} fusion(f32[1,16,4,16,16]{1,2,4,3,0:T(4,128)} %copy.269, f32[1,16,4,16,16]{1,2,4,3,0:T(4,128)} %copy.268, f32[1,16,4,16,16]{1,2,4,3,0:T(4,128)} %copy.267, f32[1,16,4,16,16]{1,2,4,3,0:T(4,128)} %copy-done.10, f32[1,16,4,16,16]{1,2,4,3,0:T(4,128)} %copy-done.9, f32[1,16,4,16,16]{1,2,4,3,0:T(4,128)} %copy-done.7, ...), kind=kOutput, calls=%fused_computation.106 | convolution fusion | flops 12976128 | bytes 1572864 | tf_op jit(solution)/shard_map/bizxy,bozxy->bioxy/dot_general | solution.py:201
  433.0 7.7 %copy.290 = f32[4,16,16,256]{3,2,1,0:T(8,128)} copy(f32[4,16,16,256]{1,2,3,0:T(8,128)} %bitcast.266) | data formatting | bytes 2097152 | tf_op jit(solution)/shard_map/reshape | solution.py:204
  440.8 6.3 %fusion.45 = f32[16,16]{0,1:T(8,128)S(1)} fusion(f32[16,32,8,128]{3,2,1,0:T(8,128)} %param.5, f32[16,32,8,128]{3,2,1,0:T(8,128)S(1)} %get-tuple-element.28), kind=kOutput, calls=%fused_computation.66 | convolution fusion | flops 100663296 | bytes 4195328 | tf_op jit(solution)/shard_map/ixys,oxys->io/dot_general | solution.py:206
  447.1 77.5 %all-reduce = (f32[16,16]{0,1:T(8,128)S(1)}, f32[16]{0:T(128)S(1)}) all-reduce(f32[16,16]{0,1:T(8,128)S(1)} %fusion.45, f32[16]{0:T(128)S(1)} %copy-done.19), channel_id=1, replica_groups=mesh['gx'=8,'gy'=32] {'gx','gy'}, use_global_device_ids=true, to_apply=%region_1.2 | all-reduce | flops 272 | bytes 2176 | tf_op jit(solution)/shard_map/psum | solution.py:210
  526.5 2.8 reshape.93
  529.3 4.8 copy.284
  534.1 2.8 copy.285
  537.7 4.1 collective-permute-done.14
  541.8 2.2 convolution_bitcast_fusion
  547.0 4.4 fusion.24
  551.4 41.4 %all-reduce.3.cloned.1.call-done = f32[4,16,16,256]{3,2,1,0:T(8,128)} async-done(((f32[4,16,16,256]{3,2,1,0:T(8,128)}), f32[4,16,16,256]{3,2,1,0:T(8,128)}) %all-reduce.3.cloned.1.call-update) | async-done | bytes 1048592 | tf_op jit(solution)/shard_map/psum | solution.py:205
  592.8 2.3 broadcast_multiply_fusion
  596.9 5.2 bitcast_add_fusion
  (169 shorter events, 71.7 us)
Async XLA Ops:
  7.2 210.0 %copy-start = (f32[16,16]{1,0:T(8,128)S(1)}, f32[16,16]{1,0:T(8,128)}, u32[]{:S(2)}) copy-start(f32[16,16]{1,0:T(8,128)} %param.8) | copy-start | bytes 3076
  9.2 6.7 %collective-permute-start = (f32[16,6,8,128]{3,1,2,0:T(8,128)S(1)}, f32[16,6,8,128]{3,1,2,0:T(8,128)S(1)}, u32[]{:S(2)}, u32[]{:S(2)}) collective-permute-start(f32[16,6,8,128]{3,1,2,0:T(8,128)S(1)} %slice.104), channel_id=1, source_target_pairs={{0,224},{32,0},{64,32},{96,64},{128,96},{160,128},{192,160},{224,1... | collective-permute-start | bytes 1179656 | tf_op jit(solution)/shard_map/ppermute | solution.py:24
  17.9 25.2 %collective-permute-start.1 = (f32[16,16,6,128]{3,1,2,0:T(8,128)S(1)}, f32[16,16,6,128]{3,1,2,0:T(8,128)S(1)}, u32[]{:S(2)}, u32[]{:S(2)}) collective-permute-start(f32[16,16,6,128]{3,1,2,0:T(8,128)S(1)} %slice.105), channel_id=1, source_target_pairs={{0,31},{1,0},{2,1},{3,2},{4,3},{5,4},{6,5},{7,6},{8,7},{9,8},{10,9... | collective-permute-start | bytes 2359304 | tf_op jit(solution)/shard_map/ppermute | solution.py:24
  49.8 12.0 %copy-start.4 = (f32[4,16,16,256]{3,2,1,0:T(8,128)S(1)}, f32[4,16,16,256]{3,2,1,0:T(8,128)}, u32[]{:S(2)}) copy-start(f32[4,16,16,256]{3,2,1,0:T(8,128)} %param.7) | copy-start | bytes 3145732
  54.1 25.3 %all-to-all-start = ((f32[32,1,4096]{2,1,0:T(1,128)}), f32[32,1,4096]{2,1,0:T(1,128)S(1)}, u32[]{:S(2)}, u32[]{:S(2)}) async-start(f32[32,1,4096]{2,1,0:T(1,128)} %reshape.86), calls=%async_computation | async-start | bytes 1048576 | tf_op jit(solution)/shard_map/all_to_all | solution.py:127
  93.2 3.9 collective-permute-start.2
  98.2 5.8 collective-permute-start.3
  100.1 224.6 %copy-start.15 = (s32[32]{0:T(128)}, s32[32]{0:T(128)S(1)}, u32[]{:S(2)}) copy-start(s32[32]{0:T(128)S(1)} %iota_multiply_fusion.3) | copy-start | bytes 388
  122.9 2.0 copy-start.5
  123.5 1.3 copy-start.7
  124.2 0.8 copy-start.8
  124.8 0.8 copy-start.9
  150.8 5.0 collective-permute-start.4
  150.9 84.3 %copy-start.11 = (s32[7]{0:T(128)}, s32[7]{0:T(128)S(1)}, u32[]{:S(2)}) copy-start(s32[7]{0:T(128)S(1)} %iota_multiply_fusion.2) | copy-start | bytes 88
  156.7 4.1 collective-permute-start.5
  156.7 10.0 %copy-start.17 = (s32[11]{0:T(128)}, s32[11]{0:T(128)S(1)}, u32[]{:S(2)}) copy-start(s32[11]{0:T(128)S(1)} %iota_multiply_fusion.1) | copy-start | bytes 136
  209.3 7.9 %copy-start.1 = (f32[16,32,8,128]{3,2,1,0:T(8,128)S(1)}, f32[16,32,8,128]{3,2,1,0:T(8,128)}, u32[]{:S(2)}) copy-start(f32[16,32,8,128]{3,2,1,0:T(8,128)} %param.5) | copy-start | bytes 6291460
  209.3 4.4 collective-permute-start.6
  209.4 10.7 %copy-start.13 = (s32[19]{0:T(128)}, s32[19]{0:T(128)S(1)}, u32[]{:S(2)}) copy-start(s32[19]{0:T(128)S(1)} %iota_multiply_fusion) | copy-start | bytes 232
  214.9 20.2 %collective-permute-start.7 = (f32[16,32,3,128]{3,1,2,0:T(8,128)S(1)}, f32[16,32,3,128]{3,1,2,0:T(8,128)S(1)}, u32[]{:S(2)}, u32[]{:S(2)}) collective-permute-start(f32[16,32,3,128]{3,1,2,0:T(8,128)S(1)} %slice.115), channel_id=1, source_target_pairs={{0,1},{1,2},{2,3},{3,4},{4,5},{5,6},{6,7},{7,8},{8,9},{9,10},{10,1... | collective-permute-start | bytes 2359304 | tf_op jit(solution)/shard_map/ppermute | solution.py:24
  220.0 15.2 %copy-start.20 = (f32[16,32,8,128]{3,2,1,0:T(8,128)S(1)}, f32[16,32,8,128]{3,2,1,0:T(8,128)}, u32[]{:S(2)}) copy-start(f32[16,32,8,128]{3,2,1,0:T(8,128)} %param.6) | copy-start | bytes 6291460
  220.0 15.2 %copy-start.21 = (f32[16]{0:T(128)S(1)}, f32[16]{0:T(128)}, u32[]{:S(2)}) copy-start(f32[16]{0:T(128)} %param.9) | copy-start | bytes 196
  241.9 5.3 collective-permute-start.8
  249.5 19.7 %collective-permute-start.9 = (f32[16,16,6,128]{3,1,2,0:T(8,128)S(1)}, f32[16,16,6,128]{3,1,2,0:T(8,128)S(1)}, u32[]{:S(2)}, u32[]{:S(2)}) collective-permute-start(f32[16,16,6,128]{3,1,2,0:T(8,128)S(1)} %slice.117), channel_id=1, source_target_pairs={{0,31},{1,0},{2,1},{3,2},{4,3},{5,4},{6,5},{7,6},{8,7},{9,8},{10,9... | collective-permute-start | bytes 2359304 | tf_op jit(solution)/shard_map/ppermute | solution.py:24
  312.2 3.9 collective-permute-start.10
  317.2 7.0 %collective-permute-start.11 = (f32[64,6,64]{2,1,0:T(8,128)S(1)}, f32[64,6,64]{2,1,0:T(8,128)S(1)}, u32[]{:S(2)}, u32[]{:S(2)}) collective-permute-start(f32[64,6,64]{2,1,0:T(8,128)S(1)} %bitcast.290), channel_id=1, source_target_pairs={{0,224},{32,0},{64,32},{96,64},{128,96},{160,128},{192,160},{224,1... | collective-permute-start | bytes 294920 | tf_op jit(solution)/shard_map/ppermute | solution.py:24
  346.1 4.4 copy-start.10
  379.3 10.5 %copy-start.12 = (s32[7]{0:T(128)S(1)}, s32[7]{0:T(128)}, u32[]{:S(2)}) copy-start(s32[7]{0:T(128)} %copy-done.11) | copy-start | bytes 88
  379.3 10.8 %copy-start.16 = (s32[32]{0:T(128)S(1)}, s32[32]{0:T(128)}, u32[]{:S(2)}) copy-start(s32[32]{0:T(128)} %copy-done.15) | copy-start | bytes 388
  381.4 13.4 %copy-start.18 = (s32[11]{0:T(128)S(1)}, s32[11]{0:T(128)}, u32[]{:S(2)}) copy-start(s32[11]{0:T(128)} %copy-done.17) | copy-start | bytes 136
  384.8 5.0 collective-permute-start.12
  390.7 4.1 collective-permute-start.13
  405.5 10.0 %copy-start.6 = (f32[1,16,4,16,16]{1,2,4,3,0:T(4,128)S(1)}, f32[1,16,4,16,16]{1,2,4,3,0:T(4,128)}, u32[]{:S(2)}) copy-start(f32[1,16,4,16,16]{1,2,4,3,0:T(4,128)} %copy-done.5) | copy-start | bytes 196612
  409.7 114.9 %all-to-all-start.3 = ((f32[32,1,4096]{2,1,0:T(1,128)}), f32[32,1,4096]{2,1,0:T(1,128)S(1)}, u32[]{:S(2)}, u32[]{:S(2)}) async-start(f32[32,1,4096]{2,1,0:T(1,128)} %reshape.92), calls=%async_computation.3 | async-start | bytes 1048576 | tf_op jit(solution)/shard_map/all_to_all | solution.py:168
  415.4 177.4 %all-reduce.3.cloned.1.call-start = ((), (), s32[]{:S(2)}) async-start(), calls=%async_computation.4 | async-start | bytes 2097152 | tf_op jit(solution)/shard_map/psum | solution.py:205
  440.8 6.3 %copy-start.19 = (f32[16]{0:T(128)S(1)}, f32[16]{0:T(128)}, u32[]{:S(2)}) copy-start(f32[16]{0:T(128)} %get-tuple-element.27) | copy-start | bytes 196
  534.1 7.7 %copy-start.14 = (s32[19]{0:T(128)S(1)}, s32[19]{0:T(128)}, u32[]{:S(2)}) copy-start(s32[19]{0:T(128)} %copy-done.13) | copy-start | bytes 232
  536.9 0.8 copy-start.3
  536.9 4.9 collective-permute-start.14
  545.0 50.1 %collective-permute-start.15 = (f32[16,32,3,128]{3,1,2,0:T(8,128)}, f32[16,32,3,128]{3,1,2,0:T(8,128)}, u32[]{:S(2)}, u32[]{:S(2)}) collective-permute-start(f32[16,32,3,128]{3,1,2,0:T(8,128)} %slice.127), channel_id=1, source_target_pairs={{0,1},{1,2},{2,3},{3,4},{4,5},{5,6},{6,7},{7,8},{8,9},{9,10},{10,1... | collective-permute-start | bytes 2359304 | tf_op jit(solution)/shard_map/ppermute | solution.py:24
  595.1 1.8 copy-start.2
Sparse Core Ops, SparseCore 0:
  440.9 151.8 all-reduce.2
where the time goes:
time: 616 us; the launch traced here: 609 us
  waiting for transfers between devices  159 us (26%)
  blocking collectives  151 us (25%)
  local copies, waits for them, and re-layouts  122 us (20%)
  matrix products  119 us (19%)
  starting transfers between devices  29.7 us (5%)
  between operations  15.3 us (2%)
  other arithmetic  13.7 us (2%)
    ppermute x16, waiting for transfers between devices, from_behind(): lax.ppermute(value, axis, [(i, (i + by) % devices) for i in range(devices)])  106 us
    psum x1, blocking collectives, local(): point_total, bias_total = lax.psum((point_local, bias_local), ('gx', 'gy'))  77.5 us
    psum x1, waiting for transfers between devices, local(): mode_total = lax.psum(mode_local, 'gy')  41.4 us
    unnamed x56, local copies, waits for them, and re-layouts  40.1 us
    all_gather x2, blocking collectives, wave_block(): gathered = lax.all_gather(level_three, 'gx', axis=1, tiled=True)  31.6 us
    all_to_all x1, blocking collectives, wave_block(): lax.all_to_all(from_lanes(delta_one, channels), 'gy', split_axis=2, conca...  22 us
    dot_general x24, matrix products, plane_y(): jnp.einsum('kr,axr->axk', matrix, signal, precision=lax.Precision.HIGHEST)  20.3 us
    all_to_all x1, blocking collectives, wave_block(): lax.all_to_all(level_one, 'gy', split_axis=3, concat_axis=2, tiled=True)  19.5 us
  transfers between devices with their start and end apart: 19, of which 17 were waited for; matrix products, arithmetic and copies ran while one was open for 11% of the time, Pallas kernels for 0%

commit v1 on v0

--- a/solution.py
+++ b/solution.py
@@ -202,7 +202,8 @@
         "bizxy,bozxy->bioxy", bands_flow, bands_grad, precision=lax.Precision.HIGHEST
     )
     mode_local = mode_local.reshape(4, channels, channels, modes_x * modes_y)
-    mode_total = lax.psum(mode_local, "gy")
+    parts = lax.all_gather(mode_local, "gy", axis=0, tiled=False)
+    mode_total = parts.sum(axis=0)
     point_local = jnp.einsum(
         "ixys,oxys->io", flow_field, grad_inner, precision=lax.Precision.HIGHEST
     )

time: 616 us -> 680 us (1.10)
  blocking collectives: 151 us -> 179 us
  other arithmetic: 13.7 us -> 30.2 us
  local copies, waits for them, and re-layouts: 122 us -> 137 us
  waiting for transfers between devices: 159 us -> 169 us
    all_gather x0 -> x1, waiting for transfers between devices: none -> 51.7 us  [local(): parts = lax.all_gather(mode_local, 'gy', axis=0, tiled=False)]
    psum x1 -> x0, waiting for transfers between devices: 41.4 us -> none  [local(): mode_total = lax.psum(mode_local, 'gy')]
    all_to_all x1 -> x2, blocking collectives: 22 us -> 48.5 us  [wave_block(): lax.all_to_all(from_lanes(delta_one, channels), 'gy', split_axis=2, conca...]
    unnamed x56 -> x44, local copies, waits for them, and re-layouts: 40.1 us -> 53.5 us
    reduce_sum x0 -> x1, other arithmetic: none -> 12.3 us  [local(): mode_total = parts.sum(axis=0)]
    reshape x1 -> x0, local copies, waits for them, and re-layouts: 7.74 us -> none  [local(): mode_local = mode_local.reshape(4, channels, channels, modes_x * modes_y)]
    another operation x0 -> x1, local copies, waits for them, and re-layouts: none -> 7.47 us  [local(): parts = lax.all_gather(mode_local, 'gy', axis=0, tiled=False)]
  transfers between devices with their start and end apart: 19 -> 18, of which waited for: 17 -> 17; matrix products, arithmetic and copies ran while one was open for 11% -> 13% of each run, Pallas kernels for 0% -> 0%
where the time goes in v1:
time: 680 us; the launch traced here: 671 us
  blocking collectives  179 us (26%)
  waiting for transfers between devices  169 us (25%)
  local copies, waits for them, and re-layouts  137 us (20%)
  matrix products  115 us (17%)
  other arithmetic  30.2 us (4%)
  starting transfers between devices  25 us (4%)
  between operations  15.5 us (2%)
    ppermute x16, waiting for transfers between devices, from_behind(): lax.ppermute(value, axis, [(i, (i + by) % devices) for i in range(devices)])  106 us
    psum x1, blocking collectives, local(): point_total, bias_total = lax.psum((point_local, bias_local), ('gx', 'gy'))  79 us
    unnamed x44, local copies, waits for them, and re-layouts  53.5 us
    all_gather x1, waiting for transfers between devices, local(): parts = lax.all_gather(mode_local, 'gy', axis=0, tiled=False)  51.7 us
    all_to_all x2, blocking collectives, wave_block(): lax.all_to_all(from_lanes(delta_one, channels), 'gy', split_axis=2, conca...  48.5 us
    all_gather x2, blocking collectives, wave_block(): gathered = lax.all_gather(level_three, 'gx', axis=1, tiled=True)  31.8 us
    dot_general x24, matrix products, plane_y(): jnp.einsum('kr,axr->axk', matrix, signal, precision=lax.Precision.HIGHEST)  21.5 us
    all_to_all x1, blocking collectives, wave_block(): lax.all_to_all(level_one, 'gy', split_axis=3, concat_axis=2, tiled=True)  19.5 us
  transfers between devices with their start and end apart: 18, of which 17 were waited for; matrix products, arithmetic and copies ran while one was open for 13% of the time, Pallas kernels for 0%

profile of v1, /device:TPU:8, one launch (start us, length us, event | category | flops | bytes accessed | tf_op | source)
XLA Modules:
  0.0 670.9 jit_solution(11738014585423525236)
XLA Ops:
  9.3 6.7 collective-permute-done
  17.9 8.1 %collective-permute-start.1 = (f32[16,16,6,128]{3,1,2,0:T(8,128)S(1)}, f32[16,16,6,128]{3,1,2,0:T(8,128)S(1)}, u32[]{:S(2)}, u32[]{:S(2)}) collective-permute-start(f32[16,16,6,128]{3,1,2,0:T(8,128)S(1)} %slice.105), channel_id=1, source_target_pairs={{0,31},{1,0},{2,1},{3,2},{4,3},{5,4},{6,5},{7,6},{8,7},{9,8},{10,9... | collective-permute-start | bytes 2359304 | tf_op jit(solution)/shard_map/ppermute | solution.py:24
  26.0 17.1 %collective-permute-done.1 = f32[16,16,6,128]{3,1,2,0:T(8,128)S(1)} collective-permute-done((f32[16,16,6,128]{3,1,2,0:T(8,128)S(1)}, f32[16,16,6,128]{3,1,2,0:T(8,128)S(1)}, u32[]{:S(2)}, u32[]{:S(2)}) %collective-permute-start.1) | collective-permute-done | bytes 786464 | tf_op jit(solution)/shard_map/ppermute | solution.py:24
  45.4 4.4 copy.209
  49.8 4.3 reshape.82
  54.1 7.5 %all-to-all-start = ((f32[32,1,4096]{2,1,0:T(1,128)}), f32[32,1,4096]{2,1,0:T(1,128)S(1)}, u32[]{:S(2)}, u32[]{:S(2)}) async-start(f32[32,1,4096]{2,1,0:T(1,128)} %reshape.82), calls=%async_computation | async-start | bytes 1048576 | tf_op jit(solution)/shard_map/all_to_all | solution.py:127
  61.8 6.2 copy.306
  68.0 11.2 %all-to-all-done = f32[32,1,4096]{2,1,0:T(1,128)S(1)} async-done(((f32[32,1,4096]{2,1,0:T(1,128)}), f32[32,1,4096]{2,1,0:T(1,128)S(1)}, u32[]{:S(2)}, u32[]{:S(2)}) %all-to-all-start) | async-done | bytes 524320 | tf_op jit(solution)/shard_map/all_to_all | solution.py:127
  81.7 2.8 reshape.83
  84.4 4.8 copy.211
  89.3 3.7 copy.212
  93.1 3.9 collective-permute-done.2
  99.9 3.9 collective-permute-done.3
  104.8 14.5 %all_gather.9 = f32[64,32,32]{0,2,1:T(8,128)S(1)} all-gather(f32[64,4,32]{0,2,1:T(8,128)S(1)} %fusion.123), channel_id=1, replica_groups=mesh['gx'=8,'gy'=32] {'gx'}, dimensions={1}, use_global_device_ids=true | all-gather | bytes 294912 | tf_op jit(solution)/shard_map/all_gather | solution.py:142
  125.7 14.6 %bitcast_subtract_fusion.1 = f32[4,16,4,16,16]{1,2,4,3,0:T(4,128)S(1)} fusion(f32[4,16,16,16,16]{2,1,4,3,0:T(8,128)} %bitcast.264, f32[1,16,4,16,16]{1,2,4,3,0:T(4,128)S(1)} %copy.227, f32[1,16,4,16,16]{1,2,4,3,0:T(4,128)S(1)} %copy.226, f32[1,16,4,16,16]{1,2,4,3,0:T(4,128)S(1)} %copy.225, f32[1,16,4,16,16]{1,2,4,3,0:T(4,128)S(1)} %copy.224), kind=kOutput, calls=%fused_computation.24 | convolution fusion | flops 13041664 | bytes 1572864 | tf_op jit(solution)/shard_map/bizxy,bioxy->bozxy/dot_general | solution.py:151
  150.8 4.8 collective-permute-done.4
  156.5 4.0 collective-permute-done.5
  162.1 4.4 copy.241
  166.6 4.7 bitcast_bitcast_fusion.1
  171.3 3.5 reshape.84
  174.8 22.1 %all_to_all.72 = f32[32,1,4096]{2,1,0:T(1,128)S(1)} all-to-all(f32[32,1,4096]{2,1,0:T(1,128)S(1)} %reshape.84), channel_id=1, replica_groups=mesh['gx'=8,'gy'=32] {'gy'}, dimensions={0} | all-to-all | bytes 1048576 | tf_op jit(solution)/shard_map/all_to_all | solution.py:168
  198.8 2.8 reshape.85
  201.6 4.8 copy.242
  206.3 2.8 copy.243
  209.2 4.4 collective-permute-done.6
  217.0 2.8 fusion.27
  219.9 15.0 %collective-permute-done.7 = f32[16,32,3,128]{3,1,2,0:T(8,128)S(1)} collective-permute-done((f32[16,32,3,128]{3,1,2,0:T(8,128)S(1)}, f32[16,32,3,128]{3,1,2,0:T(8,128)S(1)}, u32[]{:S(2)}, u32[]{:S(2)}) %collective-permute-start.7) | collective-permute-done | bytes 786464 | tf_op jit(solution)/shard_map/ppermute | solution.py:24
  235.1 6.3 fusion.1133
  241.5 5.3 collective-permute-done.8
  249.1 19.6 %collective-permute-done.9 = f32[16,16,6,128]{3,1,2,0:T(8,128)S(1)} collective-permute-done((f32[16,16,6,128]{3,1,2,0:T(8,128)S(1)}, f32[16,16,6,128]{3,1,2,0:T(8,128)S(1)}, u32[]{:S(2)}, u32[]{:S(2)}) %collective-permute-start.9) | collective-permute-done | bytes 786464 | tf_op jit(solution)/shard_map/ppermute | solution.py:24
  271.0 4.4 copy.251
  275.4 3.5 reshape.86
  278.9 19.5 %all_to_all.73 = f32[32,1,4096]{2,1,0:T(1,128)S(1)} all-to-all(f32[32,1,4096]{2,1,0:T(1,128)S(1)} %reshape.86), channel_id=1, replica_groups=mesh['gx'=8,'gy'=32] {'gy'}, dimensions={0} | all-to-all | bytes 1048576 | tf_op jit(solution)/shard_map/all_to_all | solution.py:127
  300.3 2.8 reshape.87
  303.1 4.8 copy.253
  307.9 3.7 copy.254
  311.7 3.9 collective-permute-done.10
  318.6 5.1 collective-permute-done.11
  324.6 17.3 %all_gather.10 = f32[64,32,32]{0,2,1:T(8,128)S(1)} all-gather(f32[64,4,32]{0,2,1:T(8,128)S(1)} %fusion.119), channel_id=1, replica_groups=mesh['gx'=8,'gy'=32] {'gx'}, dimensions={1}, use_global_device_ids=true | all-gather | bytes 294912 | tf_op jit(solution)/shard_map/all_gather | solution.py:142
  350.7 17.8 %fusion.86 = f32[4,16,16,16,16]{4,3,2,1,0:T(8,128)} fusion(f32[1,16,4,16,16]{1,2,4,3,0:T(4,128)} %copy.269, f32[1,16,4,16,16]{1,2,4,3,0:T(4,128)} %copy.268, f32[1,16,4,16,16]{1,2,4,3,0:T(4,128)} %copy.267, f32[1,16,4,16,16]{1,2,4,3,0:T(4,128)} %copy.266, f32[1,16,4,16,16]{1,2,4,3,0:T(4,128)} %copy-done.8, f32[1,16,4,16,16]{1,2,4,3,0:T(4,128)} %copy-done.10, ...), kind=kOutput, calls=%fused_computation.106 | convolution fusion | flops 12976128 | bytes 1572864 | tf_op jit(solution)/shard_map/bizxy,bozxy->bioxy/dot_general | solution.py:201
  368.4 7.5 %copy.290 = f32[1,4,16,16,256]{4,3,2,1,0:T(8,128)} copy(f32[1,4,16,16,256]{2,3,4,1,0:T(8,128)} %bitcast.266) | data formatting | bytes 2097152 | tf_op jit(solution)/shard_map/all_gather;reshape | solution.py:205
  375.9 17.3 %bitcast_subtract_fusion = f32[4,16,4,16,16]{1,2,4,3,0:T(4,128)S(1)} fusion(f32[4,16,16,16,16]{2,1,4,3,0:T(8,128)} %bitcast.265, f32[1,16,4,16,16]{1,2,4,3,0:T(4,128)S(1)} %copy-done.12, f32[1,16,4,16,16]{1,2,4,3,0:T(4,128)} %copy.268, f32[1,16,4,16,16]{1,2,4,3,0:T(4,128)S(1)} %copy-done.11, f32[1,16,4,16,16]{1,2,4,3,0:T(4,128)} %copy.266), kind=kOutput, calls=%fused_computation.20 | convolution fusion | flops 13041664 | bytes 1572864 | tf_op jit(solution)/shard_map/bozxy,bioxy->bizxy/dot_general | solution.py:147
  398.7 2.3 copy.271
  401.0 2.7 fusion.70
  410.4 4.8 collective-permute-done.12
  416.2 4.0 collective-permute-done.13
  421.8 4.5 copy.283
  426.2 4.9 bitcast_bitcast_fusion
  431.1 3.5 reshape.88
  434.6 26.4 %all_to_all.74 = f32[32,1,4096]{2,1,0:T(1,128)S(1)} all-to-all(f32[32,1,4096]{2,1,0:T(1,128)S(1)} %reshape.88), channel_id=1, replica_groups=mesh['gx'=8,'gy'=32] {'gy'}, dimensions={0} | all-to-all | bytes 1048576 | tf_op jit(solution)/shard_map/all_to_all | solution.py:168
  463.0 2.9 reshape.89
  465.8 4.9 copy.284
  470.8 2.8 copy.285
  474.4 3.7 collective-permute-done.14
  481.2 2.5 collective-permute-start.15
  483.7 4.8 fusion.45
  488.5 79.0 %all-reduce = (f32[16,16]{0,1:T(8,128)S(1)}, f32[16]{0:T(128)S(1)}) all-reduce(f32[16,16]{0,1:T(8,128)S(1)} %fusion.45, f32[16]{0:T(128)S(1)} %get-tuple-element.27), channel_id=1, replica_groups=mesh['gx'=8,'gy'=32] {'gx','gy'}, use_global_device_ids=true, to_apply=%region_1.2 | all-reduce | flops 272 | bytes 2176 | tf_op jit(solution)/shard_map/psum | solution.py:211
  568.7 3.1 fusion.24
  573.2 5.2 bitcast_add_fusion
  578.4 51.7 %all-gather.2.cloned.1.call-done = f32[32,4,16,16,256]{4,3,2,1,0:T(8,128)} async-done(((f32[1,4,16,16,256]{4,3,2,1,0:T(8,128)}), f32[32,4,16,16,256]{4,3,2,1,0:T(8,128)}) %all-gather.2.cloned.1.call-update) | async-done | bytes 33554448 | tf_op jit(solution)/shard_map/all_gather | solution.py:205
  630.2 12.3 %reduce_sum.18 = f32[4,16,16,256]{3,2,1,0:T(8,128)S(1)} reduce(f32[32,4,16,16,256]{4,3,2,1,0:T(8,128)} %all-gather.2.cloned.1.call-done, f32[]{:T(128)} %constant.348.clone.1), dimensions={0}, to_apply=%region_0.1 | reduce | flops 8126464 | bytes 34603012 | tf_op jit(solution)/shard_map/reduce_sum | solution.py:206
  642.5 6.3 copy.307
  648.8 7.5 %broadcast_multiply_fusion = f32[4,16,16,256]{1,2,3,0:T(8,128)} fusion(f32[4,16,16,256]{1,2,3,0:T(8,128)} %copy.307), kind=kLoop, calls=%fused_computation | loop fusion | flops 262144 | bytes 2097152 | tf_op jit(solution)/shard_map/div | solution.py:220
  656.3 7.4 %copy.294 = f32[4,16,16,256]{3,2,1,0:T(8,128)} copy(f32[4,16,16,256]{1,2,3,0:T(8,128)} %broadcast_multiply_fusion) | data formatting | bytes 2097152
  (157 shorter events, 79.8 us)
Async XLA Ops:
  7.2 209.9 %copy-start = (f32[16,16]{1,0:T(8,128)S(1)}, f32[16,16]{1,0:T(8,128)}, u32[]{:S(2)}) copy-start(f32[16,16]{1,0:T(8,128)} %param.8) | copy-start | bytes 3076
  9.2 6.7 %collective-permute-start = (f32[16,6,8,128]{3,1,2,0:T(8,128)S(1)}, f32[16,6,8,128]{3,1,2,0:T(8,128)S(1)}, u32[]{:S(2)}, u32[]{:S(2)}) collective-permute-start(f32[16,6,8,128]{3,1,2,0:T(8,128)S(1)} %slice.104), channel_id=1, source_target_pairs={{0,224},{32,0},{64,32},{96,64},{128,96},{160,128},{192,160},{224,1... | collective-permute-start | bytes 1179656 | tf_op jit(solution)/shard_map/ppermute | solution.py:24
  17.9 25.2 %collective-permute-start.1 = (f32[16,16,6,128]{3,1,2,0:T(8,128)S(1)}, f32[16,16,6,128]{3,1,2,0:T(8,128)S(1)}, u32[]{:S(2)}, u32[]{:S(2)}) collective-permute-start(f32[16,16,6,128]{3,1,2,0:T(8,128)S(1)} %slice.105), channel_id=1, source_target_pairs={{0,31},{1,0},{2,1},{3,2},{4,3},{5,4},{6,5},{7,6},{8,7},{9,8},{10,9... | collective-permute-start | bytes 2359304 | tf_op jit(solution)/shard_map/ppermute | solution.py:24
  49.8 12.0 %copy-start.5 = (f32[4,16,16,256]{3,2,1,0:T(8,128)S(1)}, f32[4,16,16,256]{3,2,1,0:T(8,128)}, u32[]{:S(2)}) copy-start(f32[4,16,16,256]{3,2,1,0:T(8,128)} %param.7) | copy-start | bytes 3145732
  54.1 25.1 %all-to-all-start = ((f32[32,1,4096]{2,1,0:T(1,128)}), f32[32,1,4096]{2,1,0:T(1,128)S(1)}, u32[]{:S(2)}, u32[]{:S(2)}) async-start(f32[32,1,4096]{2,1,0:T(1,128)} %reshape.82), calls=%async_computation | async-start | bytes 1048576 | tf_op jit(solution)/shard_map/all_to_all | solution.py:127
  61.6 568.6 %all-gather.2.cloned.1.call-start = ((), (), s32[]{:S(2)}) async-start(), calls=%async_computation.4 | async-start | bytes 34603008 | tf_op jit(solution)/shard_map/all_gather | solution.py:205
  93.0 3.9 collective-permute-start.2
  98.0 5.8 collective-permute-start.3
  122.9 2.0 copy-start.6
  123.5 1.3 copy-start.8
  124.2 0.8 copy-start.9
  124.9 0.8 copy-start.10
  150.6 5.0 collective-permute-start.4
  156.5 4.1 collective-permute-start.5
  209.1 7.9 %copy-start.1 = (f32[16,32,8,128]{3,2,1,0:T(8,128)S(1)}, f32[16,32,8,128]{3,2,1,0:T(8,128)}, u32[]{:S(2)}) copy-start(f32[16,32,8,128]{3,2,1,0:T(8,128)} %param.5) | copy-start | bytes 6291460
  209.2 4.4 collective-permute-start.6
  214.8 20.2 %collective-permute-start.7 = (f32[16,32,3,128]{3,1,2,0:T(8,128)S(1)}, f32[16,32,3,128]{3,1,2,0:T(8,128)S(1)}, u32[]{:S(2)}, u32[]{:S(2)}) collective-permute-start(f32[16,32,3,128]{3,1,2,0:T(8,128)S(1)} %slice.115), channel_id=1, source_target_pairs={{0,1},{1,2},{2,3},{3,4},{4,5},{5,6},{6,7},{7,8},{8,9},{9,10},{10,1... | collective-permute-start | bytes 2359304 | tf_op jit(solution)/shard_map/ppermute | solution.py:24
  219.9 15.2 %copy-start.13 = (f32[16,32,8,128]{3,2,1,0:T(8,128)S(1)}, f32[16,32,8,128]{3,2,1,0:T(8,128)}, u32[]{:S(2)}) copy-start(f32[16,32,8,128]{3,2,1,0:T(8,128)} %param.6) | copy-start | bytes 6291460
  219.9 15.2 %copy-start.14 = (f32[16]{0:T(128)S(1)}, f32[16]{0:T(128)}, u32[]{:S(2)}) copy-start(f32[16]{0:T(128)} %param.9) | copy-start | bytes 196
  241.4 5.3 collective-permute-start.8
  249.0 19.6 %collective-permute-start.9 = (f32[16,16,6,128]{3,1,2,0:T(8,128)S(1)}, f32[16,16,6,128]{3,1,2,0:T(8,128)S(1)}, u32[]{:S(2)}, u32[]{:S(2)}) collective-permute-start(f32[16,16,6,128]{3,1,2,0:T(8,128)S(1)} %slice.117), channel_id=1, source_target_pairs={{0,31},{1,0},{2,1},{3,2},{4,3},{5,4},{6,5},{7,6},{8,7},{9,8},{10,9... | collective-permute-start | bytes 2359304 | tf_op jit(solution)/shard_map/ppermute | solution.py:24
  311.6 3.9 collective-permute-start.10
  316.7 7.0 %collective-permute-start.11 = (f32[64,6,64]{2,1,0:T(8,128)S(1)}, f32[64,6,64]{2,1,0:T(8,128)S(1)}, u32[]{:S(2)}, u32[]{:S(2)}) collective-permute-start(f32[64,6,64]{2,1,0:T(8,128)S(1)} %bitcast.290), channel_id=1, source_target_pairs={{0,224},{32,0},{64,32},{96,64},{128,96},{160,128},{192,160},{224,1... | collective-permute-start | bytes 294920 | tf_op jit(solution)/shard_map/ppermute | solution.py:24
  346.6 4.0 copy-start.7
  368.4 7.5 %copy-start.11 = (f32[1,16,4,16,16]{1,2,4,3,0:T(4,128)S(1)}, f32[1,16,4,16,16]{1,2,4,3,0:T(4,128)}, u32[]{:S(2)}) copy-start(f32[1,16,4,16,16]{1,2,4,3,0:T(4,128)} %copy.267) | copy-start | bytes 196612
  368.4 7.5 %copy-start.12 = (f32[1,16,4,16,16]{1,2,4,3,0:T(4,128)S(1)}, f32[1,16,4,16,16]{1,2,4,3,0:T(4,128)}, u32[]{:S(2)}) copy-start(f32[1,16,4,16,16]{1,2,4,3,0:T(4,128)} %copy.269) | copy-start | bytes 196612
  401.0 5.1 copy-start.4
  410.2 5.0 collective-permute-start.12
  416.1 4.1 collective-permute-start.13
  473.6 0.8 copy-start.3
  473.6 10.1 %copy-start.2 = (f32[16,32,8,128]{3,2,1,0:T(8,128)S(1)}, f32[16,32,8,128]{3,2,1,0:T(8,128)}, u32[]{:S(2)}) copy-start(f32[16,32,8,128]{3,2,1,0:T(8,128)} %param.5) | copy-start | bytes 6291460
  473.6 4.4 collective-permute-start.14
  481.2 90.7 %collective-permute-start.15 = (f32[16,32,3,128]{3,1,2,0:T(8,128)}, f32[16,32,3,128]{3,1,2,0:T(8,128)}, u32[]{:S(2)}, u32[]{:S(2)}) collective-permute-start(f32[16,32,3,128]{3,1,2,0:T(8,128)} %slice.127), channel_id=1, source_target_pairs={{0,1},{1,2},{2,3},{3,4},{4,5},{5,6},{6,7},{7,8},{8,9},{9,10},{10,1... | collective-permute-start | bytes 2359304 | tf_op jit(solution)/shard_map/ppermute | solution.py:24
Sparse Core Ops, SparseCore 0:
  376.0 254.0 all-gather.1
